TPU v7x, 512 devices: a whole 4x4x16 slice. The times are simulated.
512 devices in a mesh: rx: 64 (over z_lo, x, core), band: 8 (over y, z_hi).
Axes of the slice: x: 4, y: 4, z: 16 (z_hi: 2, z_lo: 8; z = z_hi * 8 + z_lo), core: 2. Of those that a mesh axis runs over, the one named last changes fastest.
Arguments:
- spectra: bfloat16 [2, 256, 64, 8192], P(None, 'band', None, 'rx'), may hold values from -6 to 6
- source_index: int32 [64], replicated, may hold values from 0 to 8191, as said below
Outputs:
- stack: bfloat16 [2, 256, 64, 8192], P(None, 'band', None, 'rx')
Inputs may be any that keep to these rules, and one draw needn't show every extreme that they name: `source_index`: virtual source s is one of channels s * 128 to (s + 1) * 128 - 1; the first and the last channel are sources.
All inputs are finite; a program needn't handle non-finite values.
Results may differ from a plain program's by a relative error of at most 0.0059.
Values may be sent and summed in bfloat16 or wider, within the bound.
A program may use at most 64 MiB of HBM per device.

v0:
```python
import jax
import jax.numpy as jnp
from jax import lax
from jax.sharding import PartitionSpec as P

HALF = 4


def padded_2(block, sides, width):
    for axis, dim in sides:
        count = lax.axis_size(axis)
        forward = [(i, i + 1) for i in range(count - 1)]
        backward = [(target, source) for source, target in forward]
        low = lax.ppermute(
            lax.slice_in_dim(block, block.shape[dim] - width, None, axis=dim), axis, forward
        )
        high = lax.ppermute(lax.slice_in_dim(block, 0, width, axis=dim), axis, backward)
        block = jnp.concatenate([low, block, high], axis=dim)
    return block


def magnitude(values_in):
    values = values_in.astype(jnp.float32)
    rounded = lax.optimization_barrier(
        jnp.sqrt(values[0] * values[0] + values[1] * values[1]).astype(jnp.bfloat16)
    )
    return rounded


def whiten(spectra):
    bin_count = spectra.shape[1]
    padded = padded_2(spectra, (("band", 1),), HALF)
    amplitude = magnitude(padded).astype(jnp.float32)
    total = amplitude[0:bin_count]
    for offset in range(1, 2 * HALF + 1):
        total = total + amplitude[offset : offset + bin_count]
    smooth = total / (2 * HALF + 1)
    return (spectra.astype(jnp.float32) / (smooth + 0.1)[None]).astype(jnp.bfloat16)


def cross_spectra(whitened, source_rows):
    bin_count = whitened.shape[1]
    window_count = whitened.shape[2]
    sources = source_rows.reshape(source_rows.shape[0], 2, bin_count, window_count)
    source_real = sources[:, 0]
    source_imag = sources[:, 1]
    coefficients = jnp.stack(
        [jnp.stack([source_real, source_imag], 0), jnp.stack([-source_imag, source_real], 0)], 0
    )
    products = jnp.einsum(
        "oqnfw,qfwc->ofnc", coefficients, whitened, preferred_element_type=jnp.float32
    )
    return (products / window_count).astype(jnp.bfloat16)


def local(spectra, source_index):
    whitened = whiten(spectra)
    device_rank = lax.axis_index("rx")
    channels_here = spectra.shape[3]
    local_column = source_index[device_rank] - device_rank * channels_here
    own_row = lax.dynamic_slice_in_dim(whitened, local_column, 1, 3).reshape(1, -1)
    collected = lax.all_gather(own_row, "rx", axis=0, tiled=True)
    return cross_spectra(whitened, collected)


def solution(mesh):
    return jax.shard_map(
        local,
        mesh=mesh,
        in_specs=(P(None, "band", None, "rx"), P()),
        out_specs=P(None, "band", None, "rx"),
        check_vma=False,
    )
```

profile of v0, /device:TPU:9, one launch (start us, length us, event | category | flops | bytes accessed | tf_op | source)
XLA Modules:
  0.0 175.7 jit_solution(2140125977759759294)
XLA Ops:
  0.0 1.0 fusion.20
  1.0 15.4 %collective-permute-start = (bf16[2,4,64,128]{3,2,1,0:T(8,128)(2,1)S(1)}, bf16[2,4,64,128]{3,2,1,0:T(8,128)(2,1)S(1)}, u32[]{:S(2)}, u32[]{:S(2)}) collective-permute-start(bf16[2,4,64,128]{3,2,1,0:T(8,128)(2,1)S(1)} %get-tuple-element.7), channel_id=1, source_target_pairs={{0,1},{1,2},{2,3},{3,4},{4,5},{5,6},{6,7},{8,9},{9,10},{10,11},{11... | collective-permute-start | bytes 393224 | tf_op jit(solution)/shard_map/ppermute | solution.py:14
  16.4 1.9 %collective-permute-start.1 = (bf16[2,4,64,128]{3,2,1,0:T(8,128)(2,1)S(1)}, bf16[2,4,64,128]{3,2,1,0:T(8,128)(2,1)S(1)}, u32[]{:S(2)}, u32[]{:S(2)}) collective-permute-start(bf16[2,4,64,128]{3,2,1,0:T(8,128)(2,1)S(1)} %get-tuple-element.8), channel_id=1, source_target_pairs={{1,0},{2,1},{3,2},{4,3},{5,4},{6,5},{7,6},{9,8},{10,9},{11,10},{12... | collective-permute-start | bytes 393224 | tf_op jit(solution)/shard_map/ppermute | solution.py:17
  18.4 1.2 dynamic_slice.6
  20.3 0.0 collective-permute-done
  20.3 20.6 %collective-permute-done.1 = bf16[2,4,64,128]{3,2,1,0:T(8,128)(2,1)S(1)} collective-permute-done((bf16[2,4,64,128]{3,2,1,0:T(8,128)(2,1)S(1)}, bf16[2,4,64,128]{3,2,1,0:T(8,128)(2,1)S(1)}, u32[]{:S(2)}, u32[]{:S(2)}) %collective-permute-start.1) | collective-permute-done | bytes 131104 | tf_op jit(solution)/shard_map/ppermute | solution.py:17
  40.9 1.4 maximum_convert_fusion
  42.3 0.5 fusion.16
  42.8 0.1 convert_element_type.28
  42.9 0.0 copy-start
  43.0 0.3 fusion.14
  43.3 0.9 copy-done
  44.2 0.3 divide_convert_fusion
  44.5 0.9 dynamic-slice_reduce_fusion
  45.5 0.1 reshape.24
  45.6 121.0 %all-gather = bf16[64,1,4096]{2,1,0:T(2,128)(2,1)S(1)} all-gather(bf16[1,1,4096]{2,1,0:T(2,128)(2,1)S(1)} %reshape.24), channel_id=1, replica_groups=mesh['rx'=64,'band'=8] {'rx'}, dimensions={0}, use_global_device_ids=true | all-gather | bytes 532480 | tf_op jit(solution)/shard_map/all_gather | solution.py:62
  166.5 3.9 %reduce.1 = bf16[64,4096]{1,0:T(8,128)(2,1)} reduce(bf16[64,1,4096]{2,1,0:T(2,128)(2,1)S(1)} %all-gather, bf16[]{:T(256)} %constant.20), dimensions={1}, to_apply=%all-gather.reduce_sub_computation | reduce | bytes 1048578 | tf_op jit(solution)/shard_map/all_gather | solution.py:62
  170.5 2.1 %reshape.23 = bf16[64,2,32,64]{3,2,1,0:T(8,128)(2,1)S(1)} reshape(bf16[64,4096]{1,0:T(8,128)(2,1)} %reduce.1) | data formatting | bytes 1048576 | tf_op jit(solution)/shard_map/reshape | solution.py:44
  172.5 0.1 fusion.19
  172.6 0.2 fusion.18
  172.9 0.4 copy_bitcast_fusion
  173.3 0.4 maximum_bitcast_fusion
  173.7 1.0 fusion.7
  174.7 1.1 copy.15
Async XLA Ops:
  1.0 19.3 %collective-permute-start = (bf16[2,4,64,128]{3,2,1,0:T(8,128)(2,1)S(1)}, bf16[2,4,64,128]{3,2,1,0:T(8,128)(2,1)S(1)}, u32[]{:S(2)}, u32[]{:S(2)}) collective-permute-start(bf16[2,4,64,128]{3,2,1,0:T(8,128)(2,1)S(1)} %get-tuple-element.7), channel_id=1, source_target_pairs={{0,1},{1,2},{2,3},{3,4},{4,5},{5,6},{6,7},{8,9},{9,10},{10,11},{11... | collective-permute-start | bytes 393224 | tf_op jit(solution)/shard_map/ppermute | solution.py:14
  16.4 24.4 %collective-permute-start.1 = (bf16[2,4,64,128]{3,2,1,0:T(8,128)(2,1)S(1)}, bf16[2,4,64,128]{3,2,1,0:T(8,128)(2,1)S(1)}, u32[]{:S(2)}, u32[]{:S(2)}) collective-permute-start(bf16[2,4,64,128]{3,2,1,0:T(8,128)(2,1)S(1)} %get-tuple-element.8), channel_id=1, source_target_pairs={{1,0},{2,1},{3,2},{4,3},{5,4},{6,5},{7,6},{9,8},{10,9},{11,10},{12... | collective-permute-start | bytes 393224 | tf_op jit(solution)/shard_map/ppermute | solution.py:17
  42.9 1.2 copy-start
where the time goes:
time: 176 us
  blocking collectives  121 us (69%)
  waiting for transfers between devices  20.6 us (12%)
  starting transfers between devices  17.4 us (10%)
  local copies, waits for them, and re-layouts  7.71 us (4%)
  other arithmetic  7.3 us (4%)
    all_gather x1, blocking collectives, local(): collected = lax.all_gather(own_row, 'rx', axis=0, tiled=True)  121 us
    ppermute x1, waiting for transfers between devices, padded_2(): lax.ppermute(lax.slice_in_dim(block, 0, width, axis=dim), axis, backward)  20.6 us
    ppermute x1, starting transfers between devices, padded_2(): lax.ppermute(lax.slice_in_dim(block, block.shape[dim] - width, None, axis...  15.4 us
    all_gather x1, other arithmetic, local(): collected = lax.all_gather(own_row, 'rx', axis=0, tiled=True)  3.94 us
  transfers between devices with their start and end apart: 2, of which 1 were waited for; matrix products, arithmetic and copies ran while one was open for 1% of the time, Pallas kernels for 0%

commit v1 on v0

--- a/solution.py
+++ b/solution.py
@@ -59,7 +59,9 @@
     channels_here = spectra.shape[3]
     local_column = source_index[device_rank] - device_rank * channels_here
     own_row = lax.dynamic_slice_in_dim(whitened, local_column, 1, 3).reshape(1, -1)
-    collected = lax.all_gather(own_row, "rx", axis=0, tiled=True)
+    collected = jnp.concatenate(
+        lax.all_to_all(jnp.stack([own_row] * lax.axis_size("rx")), "rx", 0, 0), axis=0
+    )
     return cross_spectra(whitened, collected)
 
 

time: 176 us -> 108 us (0.61)
  the two profiles are of different devices: /device:TPU:9 before, /device:TPU:1 now
where the time goes in v1:
time: 108 us; the launch traced here: 107 us
  blocking collectives  45.4 us (42%)
  starting transfers between devices  17.6 us (16%)
  waiting for transfers between devices  16.2 us (15%)
  local copies, waits for them, and re-layouts  14.4 us (13%)
  other arithmetic  11.9 us (11%)
    all_to_all x1, blocking collectives, local(): lax.all_to_all(jnp.stack([own_row] * lax.axis_size('rx')), 'rx', 0, 0)  45.4 us
    ppermute x1, starting transfers between devices, padded_2(): lax.ppermute(lax.slice_in_dim(block, block.shape[dim] - width, None, axis...  16.3 us
    ppermute x1, waiting for transfers between devices, padded_2(): lax.ppermute(lax.slice_in_dim(block, 0, width, axis=dim), axis, backward)  16.2 us
    unnamed x4, local copies, waits for them, and re-layouts  5.92 us
    another operation x1, other arithmetic, local(): jnp.stack([own_row] * lax.axis_size('rx'))  4.63 us
    all_to_all x1, other arithmetic, local(): lax.all_to_all(jnp.stack([own_row] * lax.axis_size('rx')), 'rx', 0, 0)  3.94 us
  transfers between devices with their start and end apart: 2, of which 1 were waited for; matrix products, arithmetic and copies ran while one was open for 1% of the time, Pallas kernels for 0%

profile of v1, /device:TPU:1, one launch (start us, length us, event | category | flops | bytes accessed | tf_op | source)
XLA Modules:
  0.0 107.2 jit_solution(6092569536307160197)
XLA Ops:
  0.0 1.0 fusion.20
  1.0 16.3 %collective-permute-start = (bf16[2,4,64,128]{3,2,1,0:T(8,128)(2,1)S(1)}, bf16[2,4,64,128]{3,2,1,0:T(8,128)(2,1)S(1)}, u32[]{:S(2)}, u32[]{:S(2)}) collective-permute-start(bf16[2,4,64,128]{3,2,1,0:T(8,128)(2,1)S(1)} %get-tuple-element.7), channel_id=1, source_target_pairs={{0,1},{1,2},{2,3},{3,4},{4,5},{5,6},{6,7},{8,9},{9,10},{10,11},{11... | collective-permute-start | bytes 393224 | tf_op jit(solution)/shard_map/ppermute | solution.py:14
  17.3 1.3 %collective-permute-start.1 = (bf16[2,4,64,128]{3,2,1,0:T(8,128)(2,1)S(1)}, bf16[2,4,64,128]{3,2,1,0:T(8,128)(2,1)S(1)}, u32[]{:S(2)}, u32[]{:S(2)}) collective-permute-start(bf16[2,4,64,128]{3,2,1,0:T(8,128)(2,1)S(1)} %get-tuple-element.8), channel_id=1, source_target_pairs={{1,0},{2,1},{3,2},{4,3},{5,4},{6,5},{7,6},{9,8},{10,9},{11,10},{12... | collective-permute-start | bytes 393224 | tf_op jit(solution)/shard_map/ppermute | solution.py:17
  18.6 1.2 %dynamic_slice.6 = s32[1]{0:T(128)} dynamic-slice(s32[64]{0:T(128)} %param.3, s32[]{:T(128)S(6)} %select_n.6), dynamic_slice_sizes={1} | dynamic-slice | bytes 12 | tf_op jit(solution)/shard_map/dynamic_slice | solution.py:60
  20.5 16.2 %collective-permute-done.1 = bf16[2,4,64,128]{3,2,1,0:T(8,128)(2,1)S(1)} collective-permute-done((bf16[2,4,64,128]{3,2,1,0:T(8,128)(2,1)S(1)}, bf16[2,4,64,128]{3,2,1,0:T(8,128)(2,1)S(1)}, u32[]{:S(2)}, u32[]{:S(2)}) %collective-permute-start.1) | collective-permute-done | bytes 131104 | tf_op jit(solution)/shard_map/ppermute | solution.py:17
  36.7 1.4 %maximum_convert_fusion = f32[2,40,64,128]{3,2,1,0:T(8,128)S(1)} fusion(bf16[2,4,64,128]{3,2,1,0:T(8,128)(2,1)S(1)} %collective-permute-done.1, bf16[2,32,64,128]{3,2,1,0:T(8,128)(2,1)} %param.2, bf16[2,4,64,128]{3,2,1,0:T(8,128)(2,1)S(1)} %collective-permute-done), kind=kLoop, calls=%fused_computation.13 | loop fusion | flops 1966080 | bytes 3932160 | tf_op jit(solution)/shard_map/convert_element_type | solution.py:23
  38.1 0.5 fusion.16
  38.7 0.3 fusion.14
  39.1 0.9 copy-done
  40.0 0.3 divide_convert_fusion
  40.3 0.9 dynamic-slice_reduce_fusion
  41.3 1.0 stack.19
  42.4 0.6 broadcast.9
  43.0 4.6 %reduce.3 = bf16[64,4096]{1,0:T(8,128)(2,1)} reduce(bf16[64,1,4096]{2,1,0:T(2,128)(2,1)S(1)} %stack.19, bf16[]{:T(256)} %broadcast.9), dimensions={1}, to_apply=%stack.19.reduce_sub_computation | reduce | bytes 1048578 | tf_op jit(solution)/shard_map/stack | solution.py:63
  47.6 1.4 %reshape.24 = bf16[64,2,2048]{2,1,0:T(2,128)(2,1)S(1)} reshape(bf16[64,4096]{1,0:T(8,128)(2,1)} %reduce.3) | data formatting | bytes 1048576
  49.0 45.4 %all_to_all.5 = bf16[64,2,2048]{2,1,0:T(2,128)(2,1)} all-to-all(bf16[64,2,2048]{2,1,0:T(2,128)(2,1)S(1)} %reshape.24), channel_id=1, replica_groups=mesh['rx'=64,'band'=8] {'rx'}, dimensions={0} | all-to-all | bytes 1048576 | tf_op jit(solution)/shard_map/all_to_all | solution.py:63
  94.4 3.6 %reshape.25 = bf16[64,1,4096]{2,1,0:T(2,128)(2,1)S(1)} reshape(bf16[64,2,2048]{2,1,0:T(2,128)(2,1)} %all_to_all.5) | data formatting | bytes 1048576
  98.0 3.9 %reduce.1 = bf16[64,4096]{1,0:T(8,128)(2,1)} reduce(bf16[64,1,4096]{2,1,0:T(2,128)(2,1)S(1)} %reshape.25, bf16[]{:T(256)} %constant.20), dimensions={1}, to_apply=%all_to_all.3.reduce_sub_computation | reduce | bytes 1048578 | tf_op jit(solution)/shard_map/all_to_all | solution.py:63
  102.0 2.1 %reshape_reshape.3 = bf16[64,2,32,64]{3,2,1,0:T(8,128)(2,1)S(1)} reshape(bf16[64,4096]{1,0:T(8,128)(2,1)} %reduce.1) | data formatting | bytes 1048576 | tf_op jit(solution)/shard_map/reshape;reshape | solution.py:44
  104.1 0.2 fusion.18
  104.3 0.4 copy_bitcast_fusion
  104.8 0.4 maximum_bitcast_fusion
  105.2 1.0 fusion.7
  106.2 1.1 copy.15
  (5 shorter events, 0.3 us)
Async XLA Ops:
  1.0 19.5 %collective-permute-start = (bf16[2,4,64,128]{3,2,1,0:T(8,128)(2,1)S(1)}, bf16[2,4,64,128]{3,2,1,0:T(8,128)(2,1)S(1)}, u32[]{:S(2)}, u32[]{:S(2)}) collective-permute-start(bf16[2,4,64,128]{3,2,1,0:T(8,128)(2,1)S(1)} %get-tuple-element.7), channel_id=1, source_target_pairs={{0,1},{1,2},{2,3},{3,4},{4,5},{5,6},{6,7},{8,9},{9,10},{10,11},{11... | collective-permute-start | bytes 393224 | tf_op jit(solution)/shard_map/ppermute | solution.py:14
  17.3 19.4 %collective-permute-start.1 = (bf16[2,4,64,128]{3,2,1,0:T(8,128)(2,1)S(1)}, bf16[2,4,64,128]{3,2,1,0:T(8,128)(2,1)S(1)}, u32[]{:S(2)}, u32[]{:S(2)}) collective-permute-start(bf16[2,4,64,128]{3,2,1,0:T(8,128)(2,1)S(1)} %get-tuple-element.8), channel_id=1, source_target_pairs={{1,0},{2,1},{3,2},{4,3},{5,4},{6,5},{7,6},{9,8},{10,9},{11,10},{12... | collective-permute-start | bytes 393224 | tf_op jit(solution)/shard_map/ppermute | solution.py:17
  38.7 1.2 %copy-start = (bf16[2,32,64,128]{3,2,1,0:T(8,128)(2,1)S(1)}, bf16[2,32,64,128]{3,2,1,0:T(8,128)(2,1)}, u32[]{:S(2)}) copy-start(bf16[2,32,64,128]{3,2,1,0:T(8,128)(2,1)} %param.2) | copy-start | bytes 3145732
